TPU v7x, 32 devices: a whole 2x2x4 slice. The times are simulated.
32 devices in a mesh: grp: 2 (over core), gx: 4 (over z), gy: 4 (over y, x).
Axes of the slice: x: 2, y: 2, z: 4, core: 2. Of those that a mesh axis runs over, the one named last changes fastest.
Arguments:
- fields: float32 [2, 3, 128, 512], P('grp', None, 'gx', 'gy'), may hold values from -6 to 6
- coefficients: float32 [2, 128, 512], P('grp', 'gx', 'gy'), may hold values from 0.05 to 0.24
- forcing: float32 [2, 3, 128, 512], P('grp', None, 'gx', 'gy'), may hold values from -4 to 4
- element_matrix: float32 [12, 12], replicated, as said below
- source_cells: int32 [2, 1024, 128], P('grp', ('gx', 'gy')), may hold values from 0 to 4095
- target_cells: int32 [2, 1024, 128], P('grp', ('gx', 'gy')), may hold values from 0 to 4095
- peer_map: int32 [2, 1024, 1], P('grp', ('gx', 'gy')), may hold values from 0 to 15; in each aligned block of 64 rows (0 to 63, 64 to 127, ..., all dimensions but the last counted through in order) at most 8 rows name the same one
- mapping_blocks: bfloat16 [2, 1024, 128, 128], P('grp', ('gx', 'gy')), may hold values from -0.25 to 0.25
Outputs:
- new_fields: float32 [2, 3, 128, 512], P('grp', None, 'gx', 'gy')
- interface_load: float32 [2, 3, 128, 512], P('grp', None, 'gx', 'gy')
Inputs may be any that keep to these rules, and one draw needn't show every extreme that they name: `peer_map`: within the 64 blocks of one partition no receiving partition is named more than 8 times. `source_cells`: local point indices of the sending partition. `target_cells`: local point indices of the receiving partition. `element_matrix`: Symmetric; every diagonal entry exceeds the sum of magnitudes of the other entries of its row by 0.5 or more.
All inputs are finite; a program needn't handle non-finite values.
Results may differ from a plain program's by a relative error of at most 0.012.
Values sent between devices are 32-bit elements; how exact they have to be, the bound alone decides.
A program may use at most 128 MiB of HBM per device.

v0:
```python
import functools

import jax
import jax.numpy as jnp
from jax import lax
from jax.experimental import pallas as pl
from jax.experimental.pallas import tpu as pltpu
from jax.sharding import PartitionSpec as P

ITERS = 4
SUB = 4
DT_STEP = 1.0
RELAX = 0.6
ROWS = 8
LANES = 128
F32 = jnp.float32
BF16 = jnp.bfloat16


def iota(shape, dim):
    return lax.broadcasted_iota(jnp.int32, shape, dim)


def shift(value, amount, axis):
    return pltpu.roll(value, amount % value.shape[axis], axis)


def one_hot(mask):
    return jnp.where(mask, 1.0, 0.0).astype(BF16)


def flat_rows(block):
    return jnp.concatenate([block[k : k + 1] for k in range(block.shape[0])], axis=1)


def kernel(
    parts_x,
    parts_y,
    field_ref,
    coef_ref,
    force_ref,
    element_ref,
    source_ref,
    target_ref,
    peer_ref,
    map_ref,
    field_out,
    load_out,
    state,
    load,
    stat,
    row_send,
    col_send,
    row_recv,
    col_recv,
    corner_recv,
    spread,
    slot_map,
    value_send,
    value_recv,
    index_send,
    index_recv,
    halo_ss,
    halo_rs,
    value_ss,
    value_rs,
    index_ss,
    index_rs,
):
    comps, cells_x, cells_y = field_ref.shape[1:]
    links, width = source_ref.shape[1:]
    parts = parts_x * parts_y
    slots = parts * ROWS
    ext_x, ext_y = state.shape[1:]
    group = lax.axis_index("grp")
    gx = lax.axis_index("gx")
    gy = lax.axis_index("gy")
    me = gx * parts_y + gy

    def peer_device(q):
        return {"grp": 1 - group, "gx": lax.div(q, parts_y), "gy": lax.rem(q, parts_y)}

    def inside(dx, dy):
        ok = None
        for pos, step, size in ((gx, dx, parts_x), (gy, dy, parts_y)):
            if step:
                test = (pos + step >= 0) & (pos + step < size)
                ok = test if ok is None else ok & test
        return ok

    steps = ((1, 0), (-1, 0), (0, -1), (0, 1), (-1, -1), (-1, 1), (1, -1), (1, 1))

    row_send[...] = jnp.zeros_like(row_send)
    col_send[...] = jnp.zeros_like(col_send)
    row_recv[...] = jnp.zeros_like(row_recv)
    col_recv[...] = jnp.zeros_like(col_recv)
    corner_recv[...] = jnp.zeros_like(corner_recv)

    barrier = pltpu.get_barrier_semaphore()

    def greet(k, carry):
        q = lax.rem(me + k, parts)
        pl.semaphore_signal(
            barrier, inc=1, device_id=peer_device(q), device_id_type=pl.DeviceIdType.MESH
        )
        return carry

    lax.fori_loop(0, parts, greet, 0)
    for dx, dy in steps:

        @pl.when(inside(dx, dy))
        def _(dx=dx, dy=dy):
            pl.semaphore_signal(
                barrier,
                inc=1,
                device_id={"gx": gx + dx, "gy": gy + dy},
                device_id_type=pl.DeviceIdType.MESH,
            )

    beside_x = jnp.where(gx > 0, 1, 0) + jnp.where(gx < parts_x - 1, 1, 0)
    beside_y = jnp.where(gy > 0, 1, 0) + jnp.where(gy < parts_y - 1, 1, 0)
    pl.semaphore_wait(barrier, parts + (beside_x + 1) * (beside_y + 1) - 1)

    peer_col = jnp.broadcast_to(peer_ref[0].astype(F32), (links, links))
    above, across = iota((links, links), 0), iota((links, links), 1)
    peer_row = jnp.sum(jnp.where(above == across, peer_col, 0.0), axis=0, keepdims=True)
    rank = jnp.sum(
        jnp.where((peer_col == peer_row) & (above < across), 1.0, 0.0), axis=0, keepdims=True
    )
    slot_row = (peer_row * ROWS + rank).astype(jnp.int32)
    to_slot = one_hot(iota((slots, links), 0) == slot_row)
    repeat = one_hot(iota((links, links * ROWS), 0) == iota((links, links * ROWS), 1) // ROWS)
    slot_map[...] = jnp.dot(to_slot, repeat, preferred_element_type=F32).astype(BF16)
    target = target_ref[0]
    target_x = (target // cells_y).astype(F32).astype(BF16)
    target_y = (target % cells_y).astype(F32).astype(BF16)
    index = cells_y * jnp.dot(to_slot, target_x, preferred_element_type=F32)
    index = index + jnp.dot(to_slot, target_y, preferred_element_type=F32)
    index_send[...] = index.reshape(parts, ROWS, width)

    def index_copy(q, owner):
        return pltpu.make_async_remote_copy(
            src_ref=index_send.at[q],
            dst_ref=index_recv.at[owner],
            send_sem=index_ss.at[q],
            recv_sem=index_rs.at[owner],
            device_id=peer_device(q),
            device_id_type=pl.DeviceIdType.MESH,
        )

    def value_copy(q, owner, par):
        return pltpu.make_async_remote_copy(
            src_ref=value_send.at[q],
            dst_ref=value_recv.at[par, owner],
            send_sem=value_ss.at[q],
            recv_sem=value_rs.at[par, owner],
            device_id=peer_device(q),
            device_id_type=pl.DeviceIdType.MESH,
        )

    def halo_copy(d, par):
        dx, dy = steps[d]
        if d < 2:
            source, place = row_send.at[1 - d], row_recv.at[par, d]
        elif d < 4:
            source, place = col_send, col_recv.at[par, d - 2]
        else:
            edge = pl.ds(0, ROWS) if d < 6 else pl.ds(cells_x - ROWS, ROWS)
            source, place = col_send.at[edge], corner_recv.at[par, d - 4]
        return pltpu.make_async_remote_copy(
            src_ref=source,
            dst_ref=place,
            send_sem=halo_ss.at[d],
            recv_sem=halo_rs.at[par, d],
            device_id={"gx": gx + dx, "gy": gy + dy},
            device_id_type=pl.DeviceIdType.MESH,
        )

    def send_index(k, carry):
        index_copy(lax.rem(me + k, parts), me).start()
        return carry

    lax.fori_loop(0, parts, send_index, 0)

    for c in range(comps):
        state[c, :cells_x, :cells_y] = field_ref[0, c]
        load[c, :cells_x, :cells_y] = force_ref[0, c]

    ext_row = iota((ext_x, ext_y), 0)
    ext_col = iota((ext_x, ext_y), 1)
    row_at = jnp.where(ext_row < cells_x + SUB, ext_row, ext_row - ext_x) + gx * cells_x
    near = (ext_col < cells_y + SUB) | (ext_col >= ext_y - SUB)
    col_at = jnp.where(ext_col < cells_y + SUB, ext_col, ext_col - ext_y) + gy * cells_y
    keep = near & (row_at >= 0) & (row_at < cells_x * parts_x)
    keep = keep & (col_at >= 0) & (col_at < cells_y * parts_y)

    def coupling(t, carry):
        par = lax.rem(t, 2)
        centres = [state[c, :cells_x, :cells_y] for c in range(comps)]
        centres += [load[c, :cells_x, :cells_y] for c in range(comps)]
        centres.append(coef_ref[0])
        lane = iota((cells_x, cells_y), 1)
        packed = jnp.zeros((cells_x, cells_y), F32)
        for q, centre in enumerate(centres):
            row_send[0, q] = centre[:ROWS]
            row_send[1, q] = centre[cells_x - ROWS :]
            low = (lane >= 8 * q) & (lane < 8 * q + 4)
            high = (lane >= 8 * q + 4) & (lane < 8 * q + 8)
            packed = jnp.where(low, shift(centre, 8 * q, 1), packed)
            packed = jnp.where(high, shift(centre, 8 * q + 8, 1), packed)
        col_send[...] = packed
        for d, (dx, dy) in enumerate(steps):

            @pl.when(inside(dx, dy))
            def _(d=d):
                halo_copy(d, par).start()

        for d, (dx, dy) in enumerate(steps):

            @pl.when(inside(-dx, -dy))
            def _(d=d):
                halo_copy(d, par).wait_recv()

        upper = iota((ROWS, cells_y), 0) < SUB
        ends = [
            jnp.where(upper, corner_recv[par, 0], corner_recv[par, 2]),
            jnp.where(upper, corner_recv[par, 1], corner_recv[par, 3]),
        ]
        east = jnp.concatenate([col_recv[par, 0], ends[0]], axis=0)
        west = jnp.concatenate([col_recv[par, 1], ends[1]], axis=0)
        lane = iota((ext_x, cells_y), 1)
        wide = []
        for q, centre in enumerate(centres):
            end = jnp.where(upper, row_recv[par, 1, q], row_recv[par, 0, q])
            side = jnp.where(lane >= cells_y - SUB, shift(west, -8 * q - 8, 1), 0.0)
            side = jnp.where(lane < SUB, shift(east, -8 * q, 1), side)
            middle = jnp.concatenate([centre, end], axis=0)
            wide.append(jnp.where(keep, jnp.concatenate([middle, side], axis=1), 0.0))
        for c in range(comps):
            state[c] = wide[c]
            load[c] = wide[comps + c]
        coef = wide[2 * comps]

        @pl.when((t == 0) & (group == 0))
        def _():
            for k, (amount, axis) in enumerate(((-1, 0), (1, 0), (-1, 1), (1, 1))):
                stat[k] = 0.5 * (coef + shift(coef, amount, axis))

        @pl.when((t == 0) & (group == 1))
        def _():
            stat[0] = coef
            north = shift(coef, 1, 0)
            west_coef = shift(coef, 1, 1)
            corner = shift(north, 1, 1)
            for c in range(comps):
                total = 0.0
                for node, near_coef in enumerate((coef, north, west_coef, corner)):
                    k = node * comps + c
                    total = total + element_ref[k, k] * near_coef
                stat[1 + c] = RELAX / jnp.where(keep, total, 1.0)

        @pl.when(group == 0)
        def _():
            def sweep(i, carry):
                for c in range(comps):
                    v = state[c]
                    flux = load[c]
                    for k, (amount, axis) in enumerate(((-1, 0), (1, 0), (-1, 1), (1, 1))):
                        flux = flux + stat[k] * (shift(v, amount, axis) - v)
                    state[c] = jnp.where(keep, v + DT_STEP * flux, 0.0)
                return carry

            lax.fori_loop(0, SUB, sweep, 0)

        @pl.when(group == 1)
        def _():
            def sweep(i, carry):
                own = [state[c] for c in range(comps)]
                south = [shift(u, -1, 0) for u in own]
                nodal = own + south
                nodal = nodal + [shift(u, -1, 1) for u in own] + [shift(u, -1, 1) for u in south]
                stiffness = stat[0]

                def force(a):
                    total = element_ref[a, 0] * nodal[0]
                    for b in range(1, 4 * comps):
                        total = total + element_ref[a, b] * nodal[b]
                    return total * stiffness

                for c in range(comps):
                    here = force(c) + shift(force(comps + c), 1, 0)
                    there = force(2 * comps + c) + shift(force(3 * comps + c), 1, 0)
                    total = here + shift(there, 1, 1)
                    result = own[c] + (load[c] - total) * stat[1 + c]
                    state[c] = jnp.where(keep, result, 0.0)
                return carry

            lax.fori_loop(0, SUB, sweep, 0)

        table = jnp.concatenate([state[c, :cells_x, :cells_y] for c in range(comps)], axis=0)
        table = table.astype(BF16)

        def pick(i, carry):
            at = pl.multiple_of(i * ROWS, ROWS)
            source = flat_rows(source_ref[0, pl.ds(at, ROWS), :])
            span = ROWS * width
            columns = one_hot(iota((cells_y, span), 0) == source % cells_y)
            values = jnp.dot(table, columns, preferred_element_type=F32)
            in_row = iota((cells_x, span), 0) == source // cells_y
            parts_of = []
            for c in range(comps):
                chosen = jnp.where(in_row, values[c * cells_x : (c + 1) * cells_x], 0.0)
                total = chosen[:ROWS]
                for r in range(ROWS, cells_x, ROWS):
                    total = total + chosen[r : r + ROWS]
                parts_of.append(total)
            for k in range(ROWS):
                lanes = slice(k * width, (k + 1) * width)
                read = jnp.concatenate([part[:, lanes] for part in parts_of], axis=0)
                mapped = jnp.dot(read.astype(BF16), map_ref[0, at + k], preferred_element_type=F32)
                row = pl.multiple_of((at + k) * ROWS, ROWS)
                for c in range(comps):
                    spread[c, pl.ds(row, ROWS), :] = mapped[c * ROWS : (c + 1) * ROWS]
            return carry

        lax.fori_loop(0, links // ROWS, pick, 0)

        for c in range(comps):
            valued = jnp.dot(slot_map[...], spread[c].astype(BF16), preferred_element_type=F32)
            value_send[:, c] = valued.reshape(parts, ROWS, width)

        def send_value(k, carry):
            value_copy(lax.rem(me + k, parts), me, par).start()
            return carry

        lax.fori_loop(0, parts, send_value, 0)

        for d, (dx, dy) in enumerate(steps):

            @pl.when(inside(dx, dy))
            def _(d=d):
                halo_copy(d, par).wait_send()

        @pl.when(t == 0)
        def _():
            def take(k, carry):
                owner = lax.rem(me - k + parts, parts)
                index_copy(owner, owner).wait_recv()
                return carry

            lax.fori_loop(0, parts, take, 0)

        def place(k, total):
            owner = lax.rem(me - k + parts, parts)
            value_copy(owner, owner, par).wait_recv()
            where = flat_rows(index_recv[owner].astype(jnp.int32))
            span = ROWS * width
            columns = one_hot(iota((cells_y, span), 0) == where % cells_y)
            in_row = iota((cells_x, span), 0) == where // cells_y
            weighted = jnp.concatenate(
                [
                    jnp.where(in_row, flat_rows(value_recv[par, owner, c]), 0.0)
                    for c in range(comps)
                ],
                axis=0,
            ).astype(BF16)
            return total + lax.dot_general(
                weighted, columns, (((1,), (1,)), ((), ())), preferred_element_type=F32
            )

        applied = lax.fori_loop(0, parts, place, jnp.zeros((comps * cells_x, cells_y), F32))
        for c in range(comps):
            part = applied[c * cells_x : (c + 1) * cells_x]
            load_out[0, c] = part
            load[c, :cells_x, :cells_y] = force_ref[0, c] + part

        def sent(k, carry):
            value_copy(lax.rem(me + k, parts), me, par).wait_send()
            return carry

        lax.fori_loop(0, parts, sent, 0)
        return carry

    lax.fori_loop(0, ITERS, coupling, 0)

    def index_sent(k, carry):
        index_copy(lax.rem(me + k, parts), me).wait_send()
        return carry

    lax.fori_loop(0, parts, index_sent, 0)
    for c in range(comps):
        field_out[0, c] = state[c, :cells_x, :cells_y]


def body(parts_x, parts_y, fields, *rest):
    _, comps, cells_x, cells_y = fields.shape
    links, width = rest[3].shape[1:]
    parts = parts_x * parts_y
    ext = (cells_x + ROWS, cells_y + LANES)
    arrays = 2 * comps + 1
    vmem = pl.BlockSpec(memory_space=pltpu.VMEM)
    dma = pltpu.SemaphoreType.DMA
    return pl.pallas_call(
        functools.partial(kernel, parts_x, parts_y),
        out_shape=(jax.ShapeDtypeStruct(fields.shape, F32),) * 2,
        in_specs=[vmem] * 3 + [pl.BlockSpec(memory_space=pltpu.SMEM)] + [vmem] * 4,
        out_specs=(vmem, vmem),
        scratch_shapes=[
            pltpu.VMEM((comps, *ext), F32),
            pltpu.VMEM((comps, *ext), F32),
            pltpu.VMEM((4, *ext), F32),
            pltpu.VMEM((2, arrays, ROWS, cells_y), F32),
            pltpu.VMEM((cells_x, cells_y), F32),
            pltpu.VMEM((2, 2, arrays, ROWS, cells_y), F32),
            pltpu.VMEM((2, 2, cells_x, cells_y), F32),
            pltpu.VMEM((2, 4, ROWS, cells_y), F32),
            pltpu.VMEM((comps, links * ROWS, width), F32),
            pltpu.VMEM((parts * ROWS, links * ROWS), BF16),
            pltpu.VMEM((parts, comps, ROWS, width), F32),
            pltpu.VMEM((2, parts, comps, ROWS, width), F32),
            pltpu.VMEM((parts, ROWS, width), F32),
            pltpu.VMEM((parts, ROWS, width), F32),
            dma((8,)),
            dma((2, 8)),
            dma((parts,)),
            dma((2, parts)),
            dma((parts,)),
            dma((parts,)),
        ],
        compiler_params=pltpu.CompilerParams(collective_id=0, has_side_effects=True),
    )(fields, *rest)


def solution(mesh):
    placed = (
        P("grp", None, "gx", "gy"),
        P("grp", "gx", "gy"),
        P("grp", None, "gx", "gy"),
        P(),
        P("grp", ("gx", "gy"), None),
        P("grp", ("gx", "gy"), None),
        P("grp", ("gx", "gy"), None),
        P("grp", ("gx", "gy"), None, None),
    )
    return jax.shard_map(
        functools.partial(body, mesh.shape["gx"], mesh.shape["gy"]),
        mesh=mesh,
        in_specs=placed,
        out_specs=(P("grp", None, "gx", "gy"), P("grp", None, "gx", "gy")),
        check_vma=False,
    )
```

profile of v0, /device:TPU:1, one launch (start us, length us, event | category | flops | bytes accessed | tf_op | source)
XLA Modules:
  0.0 81.0 jit_solution(15764092538920014536)
XLA Ops:
  0.6 1.4 %copy.10.peer_ref = s32[1,64,1]{2,1,0:T(8,128)} copy(s32[1,64,1]{1,2,0:T(1,128)} %param.14) | data formatting | bytes 512 | tf_op args[6]
  2.0 76.1 %shard_map.95 = (f32[1,3,32,128]{3,2,1,0:T(8,128)}, f32[1,3,32,128]{3,2,1,0:T(8,128)}) custom-call(f32[1,3,32,128]{3,2,1,0:T(8,128)} %field_ref.1, f32[1,32,128]{2,1,0:T(8,128)} %coef_ref.1, f32[1,3,32,128]{3,2,1,0:T(8,128)} %force_ref.1, f32[12,12]{1,0:T(8,128)} %element_ref.1, s32[1,64,128]{2,1,0:T(8,128)} %source_ref.1, s32[1,64,128]{2,1,0:T(8,128)} %target_ref.1, ...), custom_call_target="tpu_custom_call" | custom-call | tf_op jit(solution)/shard_map/pallas_call | solution.py:403
  78.1 1.4 %copy.13 = f32[1,3,32,128]{3,2,1,0:T(8,128)} copy(f32[1,3,32,128]{3,2,1,0:T(8,128)} %get-tuple-element.4) | data formatting | bytes 98304
  79.5 1.4 %copy.14 = f32[1,3,32,128]{3,2,1,0:T(8,128)} copy(f32[1,3,32,128]{3,2,1,0:T(8,128)} %get-tuple-element.5) | data formatting | bytes 98304
where the time goes:
time: 81.2 us; the launch traced here: 81 us
  Pallas kernels  76.1 us (94%)
  local copies, waits for them, and re-layouts  4.2 us (5%)
    pallas_call x1, Pallas kernels, body(): pl.pallas_call(functools.partial(kernel, parts_x, parts_y), out_shape=(ja...  76.1 us
    unnamed x3, local copies, waits for them, and re-layouts  4.2 us

commit v1 on v0

--- a/solution.py
+++ b/solution.py
@@ -43,7 +43,7 @@
     source_ref,
     target_ref,
     peer_ref,
-    map_ref,
+    map_hbm,
     field_out,
     load_out,
     state,
@@ -66,6 +66,10 @@
     value_rs,
     index_ss,
     index_rs,
+    map_ref,
+    map_sem,
+    pick_cols,
+    place_cols,
 ):
     comps, cells_x, cells_y = field_ref.shape[1:]
     links, width = source_ref.shape[1:]
@@ -117,17 +121,14 @@
                 device_id_type=pl.DeviceIdType.MESH,
             )
 
-    beside_x = jnp.where(gx > 0, 1, 0) + jnp.where(gx < parts_x - 1, 1, 0)
-    beside_y = jnp.where(gy > 0, 1, 0) + jnp.where(gy < parts_y - 1, 1, 0)
-    pl.semaphore_wait(barrier, parts + (beside_x + 1) * (beside_y + 1) - 1)
-
-    peer_col = jnp.broadcast_to(peer_ref[0].astype(F32), (links, links))
+    pltpu.make_async_copy(map_hbm, map_ref, map_sem).start()
+    peer_row = jnp.broadcast_to(peer_ref[0].astype(F32), (links, links))
     above, across = iota((links, links), 0), iota((links, links), 1)
-    peer_row = jnp.sum(jnp.where(above == across, peer_col, 0.0), axis=0, keepdims=True)
+    peer_col = jnp.sum(jnp.where(above == across, peer_row, 0.0), axis=1, keepdims=True)
     rank = jnp.sum(
         jnp.where((peer_col == peer_row) & (above < across), 1.0, 0.0), axis=0, keepdims=True
     )
-    slot_row = (peer_row * ROWS + rank).astype(jnp.int32)
+    slot_row = (peer_row[:1] * ROWS + rank).astype(jnp.int32)
     to_slot = one_hot(iota((slots, links), 0) == slot_row)
     repeat = one_hot(iota((links, links * ROWS), 0) == iota((links, links * ROWS), 1) // ROWS)
     slot_map[...] = jnp.dot(to_slot, repeat, preferred_element_type=F32).astype(BF16)
@@ -175,6 +176,20 @@
             device_id={"gx": gx + dx, "gy": gy + dy},
             device_id_type=pl.DeviceIdType.MESH,
         )
+
+    span = ROWS * width
+
+    def prepare(i, carry):
+        at = pl.multiple_of(i * ROWS, ROWS)
+        source = flat_rows(source_ref[0, pl.ds(at, ROWS), :])
+        pick_cols[i] = one_hot(iota((cells_y, span), 0) == source % cells_y)
+        return carry
+
+    lax.fori_loop(0, links // ROWS, prepare, 0)
+
+    beside_x = jnp.where(gx > 0, 1, 0) + jnp.where(gx < parts_x - 1, 1, 0)
+    beside_y = jnp.where(gy > 0, 1, 0) + jnp.where(gy < parts_y - 1, 1, 0)
+    pl.semaphore_wait(barrier, parts + (beside_x + 1) * (beside_y + 1) - 1)
 
     def send_index(k, carry):
         index_copy(lax.rem(me + k, parts), me).start()
@@ -297,15 +312,17 @@
 
             lax.fori_loop(0, SUB, sweep, 0)
 
+        @pl.when(t == 0)
+        def _():
+            pltpu.make_async_copy(map_hbm, map_ref, map_sem).wait()
+
         table = jnp.concatenate([state[c, :cells_x, :cells_y] for c in range(comps)], axis=0)
         table = table.astype(BF16)
 
         def pick(i, carry):
             at = pl.multiple_of(i * ROWS, ROWS)
             source = flat_rows(source_ref[0, pl.ds(at, ROWS), :])
-            span = ROWS * width
-            columns = one_hot(iota((cells_y, span), 0) == source % cells_y)
-            values = jnp.dot(table, columns, preferred_element_type=F32)
+            values = jnp.dot(table, pick_cols[i], preferred_element_type=F32)
             in_row = iota((cells_x, span), 0) == source // cells_y
             parts_of = []
             for c in range(comps):
@@ -323,7 +340,7 @@
                     spread[c, pl.ds(row, ROWS), :] = mapped[c * ROWS : (c + 1) * ROWS]
             return carry
 
-        lax.fori_loop(0, links // ROWS, pick, 0)
+        lax.fori_loop(0, links // ROWS, pick, 0, unroll=4)
 
         for c in range(comps):
             valued = jnp.dot(slot_map[...], spread[c].astype(BF16), preferred_element_type=F32)
@@ -346,6 +363,9 @@
             def take(k, carry):
                 owner = lax.rem(me - k + parts, parts)
                 index_copy(owner, owner).wait_recv()
+                where = flat_rows(index_recv[owner].astype(jnp.int32))
+                mask = jnp.where(iota((cells_y, span), 0) == where % cells_y, 1.0, 0.0)
+                place_cols[owner] = mask.T.astype(BF16)
                 return carry
 
             lax.fori_loop(0, parts, take, 0)
@@ -354,8 +374,6 @@
             owner = lax.rem(me - k + parts, parts)
             value_copy(owner, owner, par).wait_recv()
             where = flat_rows(index_recv[owner].astype(jnp.int32))
-            span = ROWS * width
-            columns = one_hot(iota((cells_y, span), 0) == where % cells_y)
             in_row = iota((cells_x, span), 0) == where // cells_y
             weighted = jnp.concatenate(
                 [
@@ -365,10 +383,10 @@
                 axis=0,
             ).astype(BF16)
             return total + lax.dot_general(
-                weighted, columns, (((1,), (1,)), ((), ())), preferred_element_type=F32
+                weighted, place_cols[owner], (((1,), (0,)), ((), ())), preferred_element_type=F32
             )
 
-        applied = lax.fori_loop(0, parts, place, jnp.zeros((comps * cells_x, cells_y), F32))
+        applied = lax.fori_loop(0, parts, place, jnp.zeros((comps * cells_x, cells_y), F32), unroll=4)
         for c in range(comps):
             part = applied[c * cells_x : (c + 1) * cells_x]
             load_out[0, c] = part
@@ -390,6 +408,11 @@
     lax.fori_loop(0, parts, index_sent, 0)
     for c in range(comps):
         field_out[0, c] = state[c, :cells_x, :cells_y]
+
+
+def hand_over(field_ref, load_ref, field_out, load_out):
+    field_out[...] = field_ref[...]
+    load_out[...] = load_ref[...]
 
 
 def body(parts_x, parts_y, fields, *rest):
@@ -400,10 +423,12 @@
     arrays = 2 * comps + 1
     vmem = pl.BlockSpec(memory_space=pltpu.VMEM)
     dma = pltpu.SemaphoreType.DMA
-    return pl.pallas_call(
+    rest = (*rest[:5], rest[5].reshape(1, 1, links), rest[6])
+    results = pl.pallas_call(
         functools.partial(kernel, parts_x, parts_y),
         out_shape=(jax.ShapeDtypeStruct(fields.shape, F32),) * 2,
-        in_specs=[vmem] * 3 + [pl.BlockSpec(memory_space=pltpu.SMEM)] + [vmem] * 4,
+        in_specs=[vmem] * 3 + [pl.BlockSpec(memory_space=pltpu.SMEM)] + [vmem] * 3
+        + [pl.BlockSpec(memory_space=pl.ANY)],
         out_specs=(vmem, vmem),
         scratch_shapes=[
             pltpu.VMEM((comps, *ext), F32),
@@ -426,9 +451,16 @@
             dma((2, parts)),
             dma((parts,)),
             dma((parts,)),
+            pltpu.VMEM(rest[6].shape, BF16),
+            dma,
+            pltpu.VMEM((links // ROWS, cells_y, ROWS * width), BF16),
+            pltpu.VMEM((parts, ROWS * width, cells_y), BF16),
         ],
         compiler_params=pltpu.CompilerParams(collective_id=0, has_side_effects=True),
     )(fields, *rest)
+    return pl.pallas_call(
+        hand_over, out_shape=(jax.ShapeDtypeStruct(fields.shape, F32),) * 2, in_specs=[vmem] * 2, out_specs=(vmem, vmem)
+    )(*results)
 
 
 def solution(mesh):

time: 81.2 us -> 72.7 us (0.90)
  Pallas kernels: 76.1 us -> 71.8 us
  local copies, waits for them, and re-layouts: 4.2 us -> 0 us
    pallas_call x1, Pallas kernels: 76.1 us -> 70.3 us  [body(): pl.pallas_call(functools.partial(kernel, parts_x, parts_y), out_shape=(ja...]
    unnamed x3 -> x0, local copies, waits for them, and re-layouts: 4.2 us -> none
    pallas_call x0 -> x1, Pallas kernels: none -> 1.46 us  [body(): pl.pallas_call(hand_over, out_shape=(jax.ShapeDtypeStruct(fields.shape, F...]
where the time goes in v1:
time: 72.7 us; the launch traced here: 72.4 us
  Pallas kernels  71.8 us (99%)
    pallas_call x1, Pallas kernels, body(): pl.pallas_call(functools.partial(kernel, parts_x, parts_y), out_shape=(ja...  70.3 us
    pallas_call x1, Pallas kernels, body(): pl.pallas_call(hand_over, out_shape=(jax.ShapeDtypeStruct(fields.shape, F...  1.46 us

profile of v1, /device:TPU:1, one launch (start us, length us, event | category | flops | bytes accessed | tf_op | source)
XLA Modules:
  0.0 72.4 jit_solution(14688725331059811027)
XLA Ops:
  0.6 70.3 %shard_map.95 = (f32[1,3,32,128]{3,2,1,0:T(8,128)}, f32[1,3,32,128]{3,2,1,0:T(8,128)}) custom-call(f32[1,3,32,128]{3,2,1,0:T(8,128)} %field_ref.1, f32[1,32,128]{2,1,0:T(8,128)} %coef_ref.1, f32[1,3,32,128]{3,2,1,0:T(8,128)} %force_ref.1, f32[12,12]{1,0:T(8,128)} %element_ref.1, s32[1,64,128]{2,1,0:T(8,128)} %source_ref.1, s32[1,64,128]{2,1,0:T(8,128)} %target_ref.1, ...), custom_call_target="tpu_custom_call" | custom-call | tf_op jit(solution)/shard_map/pallas_call | solution.py:427
  71.0 1.5 %shard_map.96 = (f32[1,3,32,128]{3,2,1,0:T(8,128)}, f32[1,3,32,128]{3,2,1,0:T(8,128)}) custom-call(f32[1,3,32,128]{3,2,1,0:T(8,128)} %get-tuple-element.4.field_ref, f32[1,3,32,128]{3,2,1,0:T(8,128)} %get-tuple-element.5.load_ref), custom_call_target="tpu_custom_call" | custom-call | tf_op jit(solution)/shard_map/pallas_call | solution.py:461

commit v2 on v1

--- a/solution.py
+++ b/solution.py
@@ -84,6 +84,18 @@
     def peer_device(q):
         return {"grp": 1 - group, "gx": lax.div(q, parts_y), "gy": lax.rem(q, parts_y)}
 
+    halves = 2 if parts_x % 2 == 0 else 1
+    half = parts_x // halves
+
+    def partner_of(k, sign, across):
+        turn = lax.div(k, half * parts_y)
+        turn = halves - 1 - turn if across else turn
+        within = lax.rem(k, half * parts_y)
+        along = lax.rem(lax.rem(gx, half) + sign * lax.div(within, parts_y) + half, half)
+        x = lax.rem(lax.div(gx, half) + turn, halves) * half + along
+        y = lax.rem(gy + sign * lax.rem(within, parts_y) + parts_y, parts_y)
+        return x * parts_y + y
+
     def inside(dx, dy):
         ok = None
         for pos, step, size in ((gx, dx, parts_x), (gy, dy, parts_y)):
@@ -224,7 +236,7 @@
             packed = jnp.where(low, shift(centre, 8 * q, 1), packed)
             packed = jnp.where(high, shift(centre, 8 * q + 8, 1), packed)
         col_send[...] = packed
-        for d, (dx, dy) in enumerate(steps):
+        for d, (dx, dy) in reversed(list(enumerate(steps))):
 
             @pl.when(inside(dx, dy))
             def _(d=d):
@@ -285,7 +297,7 @@
                     state[c] = jnp.where(keep, v + DT_STEP * flux, 0.0)
                 return carry
 
-            lax.fori_loop(0, SUB, sweep, 0)
+            lax.fori_loop(0, SUB, sweep, 0, unroll=True)
 
         @pl.when(group == 1)
         def _():
@@ -310,7 +322,7 @@
                     state[c] = jnp.where(keep, result, 0.0)
                 return carry
 
-            lax.fori_loop(0, SUB, sweep, 0)
+            lax.fori_loop(0, SUB, sweep, 0, unroll=True)
 
         @pl.when(t == 0)
         def _():
@@ -347,10 +359,10 @@
             value_send[:, c] = valued.reshape(parts, ROWS, width)
 
         def send_value(k, carry):
-            value_copy(lax.rem(me + k, parts), me, par).start()
+            value_copy(partner_of(k, 1, True), me, par).start()
             return carry
 
-        lax.fori_loop(0, parts, send_value, 0)
+        lax.fori_loop(0, parts, send_value, 0, unroll=4)
 
         for d, (dx, dy) in enumerate(steps):
 
@@ -371,7 +383,7 @@
             lax.fori_loop(0, parts, take, 0)
 
         def place(k, total):
-            owner = lax.rem(me - k + parts, parts)
+            owner = partner_of(k, -1, False)
             value_copy(owner, owner, par).wait_recv()
             where = flat_rows(index_recv[owner].astype(jnp.int32))
             in_row = iota((cells_x, span), 0) == where // cells_y

time: 72.7 us -> 70.8 us (0.974)
  Pallas kernels: 71.8 us -> 69.9 us
    pallas_call x1, Pallas kernels: 70.3 us -> 68.4 us  [body(): pl.pallas_call(functools.partial(kernel, parts_x, parts_y), out_shape=(ja...]
where the time goes in v2:
time: 70.8 us; the launch traced here: 70.5 us
  Pallas kernels  69.9 us (99%)
    pallas_call x1, Pallas kernels, body(): pl.pallas_call(functools.partial(kernel, parts_x, parts_y), out_shape=(ja...  68.4 us
    pallas_call x1, Pallas kernels, body(): pl.pallas_call(hand_over, out_shape=(jax.ShapeDtypeStruct(fields.shape, F...  1.46 us

profile of v2, /device:TPU:1, one launch (start us, length us, event | category | flops | bytes accessed | tf_op | source)
XLA Modules:
  0.0 70.5 jit_solution(12644303342133501750)
XLA Ops:
  0.6 68.4 %shard_map.95 = (f32[1,3,32,128]{3,2,1,0:T(8,128)}, f32[1,3,32,128]{3,2,1,0:T(8,128)}) custom-call(f32[1,3,32,128]{3,2,1,0:T(8,128)} %field_ref.1, f32[1,32,128]{2,1,0:T(8,128)} %coef_ref.1, f32[1,3,32,128]{3,2,1,0:T(8,128)} %force_ref.1, f32[12,12]{1,0:T(8,128)} %element_ref.1, s32[1,64,128]{2,1,0:T(8,128)} %source_ref.1, s32[1,64,128]{2,1,0:T(8,128)} %target_ref.1, ...), custom_call_target="tpu_custom_call" | custom-call | tf_op jit(solution)/shard_map/pallas_call | solution.py:439
  69.1 1.5 %shard_map.96 = (f32[1,3,32,128]{3,2,1,0:T(8,128)}, f32[1,3,32,128]{3,2,1,0:T(8,128)}) custom-call(f32[1,3,32,128]{3,2,1,0:T(8,128)} %get-tuple-element.4.field_ref, f32[1,3,32,128]{3,2,1,0:T(8,128)} %get-tuple-element.5.load_ref), custom_call_target="tpu_custom_call" | custom-call | tf_op jit(solution)/shard_map/pallas_call | solution.py:473
